TPU v7x, 512 devices: a whole 4x8x8 slice. The times are simulated.
512 devices in a mesh: shards: 16 (over z, core), tensor: 4 (over x), sections: 8 (over y).
Axes of the slice: x: 4, y: 8, z: 8, core: 2. Of those that a mesh axis runs over, the one named last changes fastest.
Arguments:
- replica_grads: bfloat16 [16, 8, 2, 1536, 512], P('shards', 'sections', None, None, 'tensor'), may hold values from -6 to 6
- error_feedback: bfloat16 [16, 8, 2, 1536, 512], P('shards', 'sections', None, None, 'tensor'), may hold values from -3 to 3
- q_start: float32 [8, 2, 512, 32], P('sections', None, 'tensor'), may hold values from -0.25 to 0.25
- gram_root: float32 [8, 2, 32, 32], P('sections'), may hold values from -2 to 2
- momentum: float32 [8, 2, 1536, 512], P('sections', None, 'shards', 'tensor'), may hold values from -1.2 to 1.2
- weights: float32 [8, 2, 1536, 512], P('sections', None, 'shards', 'tensor'), may hold values from -3 to 3
- router_partials: bfloat16 [512, 1536, 40], P(('shards', 'tensor', 'sections')), may hold values from -12 to 12
- gain_partials: bfloat16 [512, 2, 1536], P(('shards', 'tensor', 'sections')), may hold values from -12 to 12
- router_momentum: float32 [1536, 40], P('shards'), may hold values from -1.2 to 1.2
- router_weights: float32 [1536, 40], P('shards'), may hold values from -3 to 3
- gain_momentum: float32 [2, 1536], P(None, 'shards'), may hold values from -1.2 to 1.2
- gain_weights: float32 [2, 1536], P(None, 'shards'), may hold values from 0.1 to 1.9
Outputs:
- new_error: bfloat16 [16, 8, 2, 1536, 512], P('shards', 'sections', None, None, 'tensor')
- new_momentum: float32 [8, 2, 1536, 512], P('sections', None, 'shards', 'tensor')
- new_weights: float32 [8, 2, 1536, 512], P('sections', None, None, 'tensor')
- new_router_momentum: float32 [1536, 40], P('shards')
- new_router_weights: float32 [1536, 40], replicated
- new_gain_momentum: float32 [2, 1536], P(None, 'shards')
- new_gain_weights: float32 [2, 1536], replicated
All inputs are finite; a program needn't handle non-finite values.
Results may differ from a plain program's by a relative error of at most 0.001.
Values sent between devices are 32-bit elements; how exact they have to be, the bound alone decides.
No kernel may reach another device: no remote copies, remote signals or barrier semaphores. Data moves between devices by JAX's collectives and lax.ppermute only.
A program may use at most 64 MiB of HBM per device.

v0:
```python
import jax
import jax.numpy as jnp
from jax import lax
from jax.sharding import PartitionSpec as P

momentum_decay = 0.9
step_size = 0.5


def per_device(
    replica_grads,
    error_feedback,
    q_start,
    gram_root,
    momentum,
    weights,
    router_partials,
    gain_partials,
    router_momentum,
    router_weights,
    gain_momentum,
    gain_weights,
):
    shard_count = lax.axis_size("shards")
    shard_index = lax.axis_index("shards")
    rows = momentum.shape[2]
    start = shard_index * rows
    highest = lax.Precision.HIGHEST
    combined = replica_grads[0].astype(jnp.float32) + error_feedback[0].astype(jnp.float32)
    p_local = jnp.einsum("ekdf,ekfr->ekdr", combined, q_start, precision=highest)
    router_term = router_partials[0].astype(jnp.float32)
    gain_term = gain_partials[0].astype(jnp.float32)
    p_total = lax.psum(p_local, ("shards", "tensor"))
    router_total, gain_total = lax.psum((router_term, gain_term), ("shards", "tensor", "sections"))
    router_rows = lax.dynamic_slice_in_dim(router_total / shard_count, start, rows, 0)
    gain_rows = lax.dynamic_slice_in_dim(gain_total / shard_count, start, rows, 1)
    p_avg = p_total / shard_count
    p_hat = jnp.einsum("ekdr,ekrt->ekdt", p_avg, gram_root, precision=highest)
    q_local = jnp.einsum("ekdf,ekdr->ekfr", combined, p_hat, precision=highest)
    q_avg = lax.psum(q_local, "shards") / shard_count
    approx = jnp.einsum("ekdr,ekfr->ekdf", p_hat, q_avg, precision=highest)
    new_error = (combined - approx).astype(jnp.bfloat16)[None]
    new_router_momentum = momentum_decay * router_momentum + router_rows
    router_part = router_weights - step_size * new_router_momentum
    new_gain_momentum = momentum_decay * gain_momentum + gain_rows
    gain_part = gain_weights - step_size * new_gain_momentum
    approx_rows = lax.dynamic_slice_in_dim(approx, start, rows, 2)
    new_momentum = momentum_decay * momentum + approx_rows
    weight_rows = weights - step_size * new_momentum
    new_weights, new_router_weights, new_gain_weights = (
        lax.all_gather(weight_rows, "shards", axis=2, tiled=True),
        lax.all_gather(router_part, "shards", axis=0, tiled=True),
        lax.all_gather(gain_part, "shards", axis=1, tiled=True),
    )
    return (
        new_error,
        new_momentum,
        new_weights,
        new_router_momentum,
        new_router_weights,
        new_gain_momentum,
        new_gain_weights,
    )


def solution(mesh):
    return jax.shard_map(
        per_device,
        mesh=mesh,
        in_specs=(
            P("shards", "sections", None, None, "tensor"),
            P("shards", "sections", None, None, "tensor"),
            P("sections", None, "tensor", None),
            P("sections", None, None, None),
            P("sections", None, "shards", "tensor"),
            P("sections", None, "shards", "tensor"),
            P(("shards", "tensor", "sections"), None, None),
            P(("shards", "tensor", "sections"), None, None),
            P("shards", None),
            P("shards", None),
            P(None, "shards"),
            P(None, "shards"),
        ),
        out_specs=(
            P("shards", "sections", None, None, "tensor"),
            P("sections", None, "shards", "tensor"),
            P("sections", None, None, "tensor"),
            P("shards", None),
            P(),
            P(None, "shards"),
            P(),
        ),
        check_vma=False,
    )
```

profile of v0, /device:TPU:1, one launch (start us, length us, event | category | flops | bytes accessed | tf_op | source)
XLA Modules:
  0.0 531.9 jit_solution(9592228355170978360)
XLA Ops:
  7.3 0.7 copy-done
  7.9 3.9 convolution_bitcast_fusion
  11.9 0.0 all-reduce.5.cloned.1.call-start
  11.9 0.7 bitcast_convert_fusion
  12.7 0.0 all-gather.4.cloned.1.call-start
  12.7 195.2 %all-reduce.3.cloned.1.call-done = f32[1,2,1536,32]{2,3,1,0:T(8,128)} async-done(((f32[1,2,1536,32]{2,3,1,0:T(8,128)}), f32[1,2,1536,32]{2,3,1,0:T(8,128)}) %all-reduce.3.cloned.1.call-update) | async-done | bytes 393232 | tf_op jit(solution)/shard_map/psum | solution.py:33
  207.9 1.5 fusion.8
  209.4 0.7 copy-done.3
  210.2 1.1 fusion.4
  211.4 46.7 %psum.29 = f32[1,2,128,32]{2,3,1,0:T(8,128)S(1)} all-reduce(f32[1,2,128,32]{2,3,1,0:T(8,128)S(1)} %fusion.4), channel_id=1, replica_groups=mesh['shards'=16,'tensor'=4,'sections'=8] {'shards'}, use_global_device_ids=true, to_apply=%region_1.0 | all-reduce | flops 8192 | bytes 65536 | tf_op jit(solution)/shard_map/psum | solution.py:40
  258.0 3.6 fusion.12
  261.7 0.7 multiply_subtract_fusion
  262.4 99.3 %psum.31 = f32[2,1536]{1,0:T(2,128)S(1)} all-reduce(f32[2,1536]{1,0:T(2,128)S(1)} %bitcast_convert_fusion.1), channel_id=1, replica_groups=mesh['shards'=16,'tensor'=4,'sections'=8] {'shards','tensor','sections'}, use_global_device_ids=true, to_apply=%region_3.0 | all-reduce | flops 3072 | bytes 24576 | tf_op jit(solution)/shard_map/psum | solution.py:34
  361.8 0.6 subtract_bitcast_fusion.1
  362.4 16.6 %all-gather.1 = f32[16,96,2]{1,2,0:T(2,128)S(1)} all-gather(f32[1,96,2]{1,2,0:T(2,128)S(1)} %get-tuple-element.7), channel_id=1, replica_groups=mesh['shards'=16,'tensor'=4,'sections'=8] {'shards'}, dimensions={0}, use_global_device_ids=true | all-gather | bytes 13056 | tf_op jit(solution)/shard_map/all_gather | solution.py:53
  379.0 0.7 reshape.67
  379.7 101.5 %all-reduce.5.cloned.1.call-done = f32[1536,40]{0,1:T(8,128)} async-done(((f32[1536,40]{0,1:T(8,128)}), f32[1536,40]{0,1:T(8,128)}) %all-reduce.5.cloned.1.call-update) | async-done | bytes 245776 | tf_op jit(solution)/shard_map/psum | solution.py:34
  481.2 1.5 subtract_bitcast_fusion
  482.6 17.2 %all-gather = f32[16,96,40]{1,2,0:T(8,128)S(1)} all-gather(f32[1,96,40]{1,2,0:T(8,128)S(1)} %get-tuple-element.9), channel_id=1, replica_groups=mesh['shards'=16,'tensor'=4,'sections'=8] {'shards'}, dimensions={0}, use_global_device_ids=true | all-gather | bytes 261120 | tf_op jit(solution)/shard_map/all_gather | solution.py:52
  499.9 0.1 copy.24
  499.9 0.9 reshape.65
  500.8 1.1 fusion.7
  501.9 20.8 %all-gather.4.cloned.1.call-done = f32[1,2,1536,128]{3,2,1,0:T(8,128)} async-done(((f32[1,2,96,128]{3,2,1,0:T(8,128)}), f32[1,2,1536,128]{3,2,1,0:T(8,128)}) %all-gather.4.cloned.1.call-update) | async-done | bytes 1572880 | tf_op jit(solution)/shard_map/all_gather | solution.py:51
  522.7 2.7 copy.30
  (30 shorter events, 0.2 us)
Async XLA Ops:
  7.2 0.8 copy-start
  7.2 203.0 %copy-start.1 = (bf16[1,1,2,1536,128]{4,3,2,1,0:T(8,128)(2,1)S(1)}, bf16[1,1,2,1536,128]{4,3,2,1,0:T(8,128)(2,1)}, u32[]{:S(2)}) copy-start(bf16[1,1,2,1536,128]{4,3,2,1,0:T(8,128)(2,1)} %param.13) | copy-start | bytes 2359300
  7.2 203.0 %copy-start.2 = (bf16[1,1,2,1536,128]{4,3,2,1,0:T(8,128)(2,1)S(1)}, bf16[1,1,2,1536,128]{4,3,2,1,0:T(8,128)(2,1)}, u32[]{:S(2)}) copy-start(bf16[1,1,2,1536,128]{4,3,2,1,0:T(8,128)(2,1)} %param.12) | copy-start | bytes 2359300
  7.2 4.7 copy-start.4
  7.2 200.7 %copy-start.7 = (f32[1,2,32,32]{3,2,1,0:T(8,128)S(1)}, f32[1,2,32,32]{3,2,1,0:T(8,128)}, u32[]{:S(2)}) copy-start(f32[1,2,32,32]{3,2,1,0:T(8,128)} %param.15) | copy-start | bytes 24580
  7.2 200.7 %all-reduce.3.cloned.1.call-start = ((), (), s32[]{:S(2)}) async-start(), calls=%async_computation | async-start | bytes 786432 | tf_op jit(solution)/shard_map/psum | solution.py:33
  11.9 469.3 %all-reduce.5.cloned.1.call-start = ((), (), s32[]{:S(2)}) async-start(), calls=%async_computation.2 | async-start | bytes 491520 | tf_op jit(solution)/shard_map/psum | solution.py:34
  12.7 510.0 %all-gather.4.cloned.1.call-start = ((), (), s32[]{:S(2)}) async-start(), calls=%async_computation.1 | async-start | bytes 1671168 | tf_op jit(solution)/shard_map/all_gather | solution.py:51
  209.4 0.7 copy-start.3
  210.2 51.5 %copy-start.5 = (f32[1,2,96,128]{3,2,1,0:T(8,128)S(1)}, f32[1,2,96,128]{3,2,1,0:T(8,128)}, u32[]{:S(2)}) copy-start(f32[1,2,96,128]{3,2,1,0:T(8,128)} %param.17) | copy-start | bytes 294916
  210.2 51.5 %copy-start.6 = (f32[1,2,96,128]{3,2,1,0:T(8,128)S(1)}, f32[1,2,96,128]{3,2,1,0:T(8,128)}, u32[]{:S(2)}) copy-start(f32[1,2,96,128]{3,2,1,0:T(8,128)} %param.16) | copy-start | bytes 294916
  211.3 51.1 %copy-start.10 = (bf16[1,2,1536]{2,1,0:T(2,128)(2,1)S(1)}, bf16[1,2,1536]{2,1,0:T(2,128)(2,1)}, u32[]{:S(2)}) copy-start(bf16[1,2,1536]{2,1,0:T(2,128)(2,1)} %param.19) | copy-start | bytes 18436
  211.3 150.4 %copy-start.11 = (f32[2,96]{1,0:T(2,128)S(1)}, f32[2,96]{1,0:T(2,128)}, u32[]{:S(2)}) copy-start(f32[2,96]{1,0:T(2,128)} %param.23) | copy-start | bytes 2308
  211.3 150.4 %copy-start.12 = (f32[2,96]{1,0:T(2,128)S(1)}, f32[2,96]{1,0:T(2,128)}, u32[]{:S(2)}) copy-start(f32[2,96]{1,0:T(2,128)} %param.22) | copy-start | bytes 2308
  211.4 269.8 %copy-start.8 = (f32[96,40]{0,1:T(8,128)S(1)}, f32[96,40]{0,1:T(8,128)}, u32[]{:S(2)}) copy-start(f32[96,40]{0,1:T(8,128)} %param.21) | copy-start | bytes 46084
  211.4 269.8 %copy-start.9 = (f32[96,40]{0,1:T(8,128)S(1)}, f32[96,40]{0,1:T(8,128)}, u32[]{:S(2)}) copy-start(f32[96,40]{0,1:T(8,128)} %param.20) | copy-start | bytes 46084
Sparse Core Ops, SparseCore 0:
  12.1 195.7 all-reduce.2
  214.2 266.8 all-reduce.4
  483.9 38.7 all-gather.3
where the time goes:
time: 532 us
  waiting for transfers between devices  317 us (60%)
  blocking collectives  180 us (34%)
  between operations  13.9 us (3%)
  matrix products  10.2 us (2%)
  local copies, waits for them, and re-layouts  5.72 us (1%)
    psum x1, waiting for transfers between devices, per_device(): p_total = lax.psum(p_local, ('shards', 'tensor'))  195 us
    psum x1, waiting for transfers between devices, per_device(): lax.psum((router_term, gain_term), ('shards', 'tensor', 'sections'))  101 us
    psum x1, blocking collectives, per_device(): lax.psum((router_term, gain_term), ('shards', 'tensor', 'sections'))  99.3 us
    psum x1, blocking collectives, per_device(): q_avg = lax.psum(q_local, 'shards') / shard_count  46.7 us
    all_gather x1, waiting for transfers between devices, per_device(): lax.all_gather(weight_rows, 'shards', axis=2, tiled=True)  20.8 us
    all_gather x1, blocking collectives, per_device(): lax.all_gather(router_part, 'shards', axis=0, tiled=True)  17.2 us
    all_gather x1, blocking collectives, per_device(): lax.all_gather(gain_part, 'shards', axis=1, tiled=True)  16.6 us
  transfers between devices with their start and end apart: 3, of which 3 were waited for; matrix products, arithmetic and copies ran while one was open for 2% of the time, Pallas kernels for 0%

commit v1 on v0

--- a/solution.py
+++ b/solution.py
@@ -30,7 +30,7 @@
     p_local = jnp.einsum("ekdf,ekfr->ekdr", combined, q_start, precision=highest)
     router_term = router_partials[0].astype(jnp.float32)
     gain_term = gain_partials[0].astype(jnp.float32)
-    p_total = lax.psum(p_local, ("shards", "tensor"))
+    p_total = jnp.sum(lax.all_gather(p_local, ("shards", "tensor")), axis=0)
     router_total, gain_total = lax.psum((router_term, gain_term), ("shards", "tensor", "sections"))
     router_rows = lax.dynamic_slice_in_dim(router_total / shard_count, start, rows, 0)
     gain_rows = lax.dynamic_slice_in_dim(gain_total / shard_count, start, rows, 1)

time: 532 us -> 358 us (0.67)
  waiting for transfers between devices: 317 us -> 136 us
  other arithmetic: 4.67 us -> 14.4 us
    psum x1 -> x0, waiting for transfers between devices: 195 us -> none  [per_device(): p_total = lax.psum(p_local, ('shards', 'tensor'))]
    all_gather x0 -> x1, waiting for transfers between devices: none -> 133 us  [per_device(): p_total = jnp.sum(lax.all_gather(p_local, ('shards', 'tensor')), axis=0)]
    psum x1, waiting for transfers between devices: 101 us -> 2.91 us  [per_device(): lax.psum((router_term, gain_term), ('shards', 'tensor', 'sections'))]
    all_gather x1, waiting for transfers between devices: 20.8 us -> 0.01 us  [per_device(): lax.all_gather(weight_rows, 'shards', axis=2, tiled=True)]
    reduce_sum x0 -> x1, other arithmetic: none -> 9.74 us  [per_device(): p_total = jnp.sum(lax.all_gather(p_local, ('shards', 'tensor')), axis=0)]
  transfers between devices with their start and end apart: 3 -> 3, of which waited for: 3 -> 2; matrix products, arithmetic and copies ran while one was open for 2% -> 6% of each run, Pallas kernels for 0% -> 0%
where the time goes in v1:
time: 358 us; the launch traced here: 357 us
  blocking collectives  176 us (49%)
  waiting for transfers between devices  136 us (38%)
  between operations  15.6 us (4%)
  other arithmetic  14.4 us (4%)
  matrix products  9.17 us (3%)
  local copies, waits for them, and re-layouts  5.75 us (2%)
    all_gather x1, waiting for transfers between devices, per_device(): p_total = jnp.sum(lax.all_gather(p_local, ('shards', 'tensor')), axis=0)  133 us
    psum x1, blocking collectives, per_device(): lax.psum((router_term, gain_term), ('shards', 'tensor', 'sections'))  99.2 us
    psum x1, blocking collectives, per_device(): q_avg = lax.psum(q_local, 'shards') / shard_count  44.3 us
    all_gather x1, blocking collectives, per_device(): lax.all_gather(router_part, 'shards', axis=0, tiled=True)  17.3 us
    all_gather x1, blocking collectives, per_device(): lax.all_gather(gain_part, 'shards', axis=1, tiled=True)  15.5 us
    reduce_sum x1, other arithmetic, per_device(): p_total = jnp.sum(lax.all_gather(p_local, ('shards', 'tensor')), axis=0)  9.74 us
  transfers between devices with their start and end apart: 3, of which 2 were waited for; matrix products, arithmetic and copies ran while one was open for 6% of the time, Pallas kernels for 0%

profile of v1, /device:TPU:1, one launch (start us, length us, event | category | flops | bytes accessed | tf_op | source)
XLA Modules:
  0.0 357.1 jit_solution(1043170156474543315)
XLA Ops:
  8.1 0.7 copy-done
  8.8 3.9 %fusion.2 = f32[2,1536,32]{1,2,0:T(8,128)} fusion(bf16[1,1,2,1536,128]{4,3,2,1,0:T(8,128)(2,1)} %param.13, bf16[1,1,2,1536,128]{4,3,2,1,0:T(8,128)(2,1)} %param.12, f32[1,2,128,32]{2,3,1,0:T(8,128)S(1)} %copy-done), kind=kOutput, calls=%fused_computation.3 | convolution fusion | flops 152174592 | bytes 1998848 | tf_op jit(solution)/shard_map/ekdf,ekfr->ekdr/dot_general | solution.py:30
  12.7 0.0 all-reduce.2.cloned.1.call-start
  12.8 0.7 bitcast_convert_fusion
  13.5 0.0 all-gather.6.cloned.1.call-start
  13.6 132.9 %all-gather.8.cloned.1.call-done = f32[128,1536,32]{1,2,0:T(8,128)} async-done(((f32[2,1536,32]{1,2,0:T(8,128)}), f32[128,1536,32]{1,2,0:T(8,128)}) %all-gather.8.cloned.1.call-update) | async-done | bytes 25165840 | tf_op jit(solution)/shard_map/all_gather | solution.py:33
  146.4 9.7 %reduce.1 = f32[2,1536,32]{1,2,0:T(8,128)S(1)} reduce(f32[64,2,1536,32]{2,3,1,0:T(8,128)} %bitcast.48, f32[]{:T(128)} %constant.9.clone.1), dimensions={0}, to_apply=%region_0.0 | reduce | flops 6193152 | bytes 25559044 | tf_op jit(solution)/shard_map/reduce_sum | solution.py:33
  156.2 0.5 fusion.9
  156.7 0.7 copy-done.3
  157.5 1.1 fusion.5
  158.7 44.3 %psum.21 = f32[1,2,128,32]{2,3,1,0:T(8,128)S(1)} all-reduce(f32[1,2,128,32]{2,3,1,0:T(8,128)S(1)} %fusion.5), channel_id=1, replica_groups=mesh['shards'=16,'tensor'=4,'sections'=8] {'shards'}, use_global_device_ids=true, to_apply=%region_1.0 | all-reduce | flops 8192 | bytes 65536 | tf_op jit(solution)/shard_map/psum | solution.py:40
  202.9 3.6 %fusion.12 = f32[2,1536,128]{2,1,0:T(8,128)S(1)} fusion(f32[2,1536,32]{1,2,0:T(8,128)} %copy-done.3, f32[1,2,128,32]{2,3,1,0:T(8,128)S(1)} %psum.21), kind=kOutput, calls=%fused_computation.15 | convolution fusion | flops 151003136 | bytes 1998848 | tf_op jit(solution)/shard_map/ekdr,ekfr->ekdf/dot_general | solution.py:41
  206.6 0.7 multiply_subtract_fusion
  207.3 99.2 %psum.23 = f32[2,1536]{1,0:T(2,128)S(1)} all-reduce(f32[2,1536]{1,0:T(2,128)S(1)} %bitcast_convert_fusion.1), channel_id=1, replica_groups=mesh['shards'=16,'tensor'=4,'sections'=8] {'shards','tensor','sections'}, use_global_device_ids=true, to_apply=%region_3.0 | all-reduce | flops 3072 | bytes 24576 | tf_op jit(solution)/shard_map/psum | solution.py:34
  306.5 0.6 subtract_bitcast_fusion.1
  307.1 15.5 %all-gather.2 = f32[16,96,2]{1,2,0:T(2,128)S(1)} all-gather(f32[1,96,2]{1,2,0:T(2,128)S(1)} %get-tuple-element.7), channel_id=1, replica_groups=mesh['shards'=16,'tensor'=4,'sections'=8] {'shards'}, dimensions={0}, use_global_device_ids=true | all-gather | bytes 13056 | tf_op jit(solution)/shard_map/all_gather | solution.py:53
  322.6 0.7 reshape.72
  323.3 2.9 all-reduce.2.cloned.1.call-done
  326.2 1.5 subtract_bitcast_fusion
  327.7 17.3 %all-gather.1 = f32[16,96,40]{1,2,0:T(8,128)S(1)} all-gather(f32[1,96,40]{1,2,0:T(8,128)S(1)} %get-tuple-element.9), channel_id=1, replica_groups=mesh['shards'=16,'tensor'=4,'sections'=8] {'shards'}, dimensions={0}, use_global_device_ids=true | all-gather | bytes 261120 | tf_op jit(solution)/shard_map/all_gather | solution.py:52
  345.0 0.1 copy.24
  345.0 0.9 reshape.70
  345.9 1.1 fusion.8
  347.0 2.7 copy.29
  (31 shorter events, 0.2 us)
Async XLA Ops:
  8.0 0.8 copy-start
  8.0 4.7 %copy-start.4 = (bf16[1,1536,40]{1,2,0:T(8,128)(2,1)S(1)}, bf16[1,1536,40]{1,2,0:T(8,128)(2,1)}, u32[]{:S(2)}) copy-start(bf16[1,1536,40]{1,2,0:T(8,128)(2,1)} %param.18) | copy-start | bytes 368644
  8.0 138.4 %all-gather.8.cloned.1.call-start = ((), (), s32[]{:S(2)}) async-start(), calls=%async_computation.2 | async-start | bytes 25559040 | tf_op jit(solution)/shard_map/all_gather | solution.py:33
  12.7 313.5 %all-reduce.2.cloned.1.call-start = ((), (), s32[]{:S(2)}) async-start(), calls=%async_computation.1 | async-start | bytes 491520 | tf_op jit(solution)/shard_map/psum | solution.py:34
  13.5 333.5 %all-gather.6.cloned.1.call-start = ((), (), s32[]{:S(2)}) async-start(), calls=%async_computation | async-start | bytes 1671168 | tf_op jit(solution)/shard_map/all_gather | solution.py:51
  146.4 9.8 %copy-start.7 = (f32[1,2,32,32]{3,2,1,0:T(8,128)S(1)}, f32[1,2,32,32]{3,2,1,0:T(8,128)}, u32[]{:S(2)}) copy-start(f32[1,2,32,32]{3,2,1,0:T(8,128)} %param.15) | copy-start | bytes 24580
  146.4 11.0 %copy-start.1 = (bf16[1,1,2,1536,128]{4,3,2,1,0:T(8,128)(2,1)S(1)}, bf16[1,1,2,1536,128]{4,3,2,1,0:T(8,128)(2,1)}, u32[]{:S(2)}) copy-start(bf16[1,1,2,1536,128]{4,3,2,1,0:T(8,128)(2,1)} %param.13) | copy-start | bytes 2359300
  146.4 11.0 %copy-start.2 = (bf16[1,1,2,1536,128]{4,3,2,1,0:T(8,128)(2,1)S(1)}, bf16[1,1,2,1536,128]{4,3,2,1,0:T(8,128)(2,1)}, u32[]{:S(2)}) copy-start(bf16[1,1,2,1536,128]{4,3,2,1,0:T(8,128)(2,1)} %param.12) | copy-start | bytes 2359300
  156.7 0.7 copy-start.3
  157.4 49.1 %copy-start.5 = (f32[1,2,96,128]{3,2,1,0:T(8,128)S(1)}, f32[1,2,96,128]{3,2,1,0:T(8,128)}, u32[]{:S(2)}) copy-start(f32[1,2,96,128]{3,2,1,0:T(8,128)} %param.17) | copy-start | bytes 294916
  157.4 49.1 %copy-start.6 = (f32[1,2,96,128]{3,2,1,0:T(8,128)S(1)}, f32[1,2,96,128]{3,2,1,0:T(8,128)}, u32[]{:S(2)}) copy-start(f32[1,2,96,128]{3,2,1,0:T(8,128)} %param.16) | copy-start | bytes 294916
  158.6 48.7 %copy-start.10 = (bf16[1,2,1536]{2,1,0:T(2,128)(2,1)S(1)}, bf16[1,2,1536]{2,1,0:T(2,128)(2,1)}, u32[]{:S(2)}) copy-start(bf16[1,2,1536]{2,1,0:T(2,128)(2,1)} %param.19) | copy-start | bytes 18436
  158.6 147.9 %copy-start.11 = (f32[2,96]{1,0:T(2,128)S(1)}, f32[2,96]{1,0:T(2,128)}, u32[]{:S(2)}) copy-start(f32[2,96]{1,0:T(2,128)} %param.23) | copy-start | bytes 2308
  158.6 147.9 %copy-start.12 = (f32[2,96]{1,0:T(2,128)S(1)}, f32[2,96]{1,0:T(2,128)}, u32[]{:S(2)}) copy-start(f32[2,96]{1,0:T(2,128)} %param.22) | copy-start | bytes 2308
  158.6 167.6 %copy-start.8 = (f32[96,40]{0,1:T(8,128)S(1)}, f32[96,40]{0,1:T(8,128)}, u32[]{:S(2)}) copy-start(f32[96,40]{0,1:T(8,128)} %param.21) | copy-start | bytes 46084
  158.6 167.6 %copy-start.9 = (f32[96,40]{0,1:T(8,128)S(1)}, f32[96,40]{0,1:T(8,128)}, u32[]{:S(2)}) copy-start(f32[96,40]{0,1:T(8,128)} %param.20) | copy-start | bytes 46084
Sparse Core Ops, SparseCore 0:
  12.8 133.5 all-gather.7
  207.4 43.0 all-gather.5
Sparse Core Ops, SparseCore 1:
  18.7 307.4 all-reduce.1
